TPU v7x, 32 devices: a whole 2x2x4 slice. The times are simulated.
32 devices in a mesh: groups: 2 (over y), seq: 4 (over z), section: 2 (over x), tp: 2 (over core).
Axes of the slice: x: 2, y: 2, z: 4, core: 2. Of those that a mesh axis runs over, the one named last changes fastest.
Arguments:
- hidden_in: bfloat16 [16, 8192], P('groups', ('seq', 'section', 'tp')), parts along dimension 0, may hold values from -6 to 6
- lengths: int32 [16], P('groups'), parts along dimension 0, may hold values from 1 to 512, as said below
- key_value_cache: bfloat16 [16, 2, 512, 1024], P('groups', None, 'seq', ('section', 'tp')), parts along dimension 0, may hold values from -900 to 900
- attn_gain: float32 [8192], P('seq'), may hold values from 0.1 to 1.9
- w_query: bfloat16 [8192, 8192], P('seq', ('section', 'tp')), may hold values from -0.0625 to 0.0625
- key_value_weight: bfloat16 [8192, 2, 1024], P('seq', None, ('section', 'tp')), may hold values from -0.0625 to 0.0625
- w_output: bfloat16 [8192, 8192], P(('section', 'tp'), 'seq'), may hold values from -0.0625 to 0.0625
- mamba_gain: float32 [8192], P('seq'), may hold values from 0.1 to 1.9
- w_inproj: bfloat16 [8192, 2, 16384], P('seq', None, ('section', 'tp')), may hold values from -0.09375 to 0.09375
- conv_weight: float32 [4, 16384], P(None, ('section', 'tp', 'seq')), may hold values from -3 to 3
- conv_bias: float32 [16384], P(('section', 'tp', 'seq')), may hold values from -3 to 3
- w_xproj: bfloat16 [16384, 544], P(('section', 'tp', 'seq')), may hold values from -0.046875 to 0.046875
- w_dtproj: bfloat16 [512, 16384], P(None, ('section', 'tp', 'seq')), may hold values from -0.25 to 0.25
- dt_bias: float32 [16384], P(('section', 'tp', 'seq')), may hold values from -4 to 0
- a_log: float32 [16, 16384], P(None, ('section', 'tp', 'seq')), may hold values from 0 to 2.77
- d_skip: float32 [16384], P(('section', 'tp', 'seq')), may hold values from 0.25 to 2
- w_outproj: bfloat16 [16384, 8192], P(('section', 'tp'), 'seq'), may hold values from -0.046875 to 0.046875
- ssm_state: float32 [16, 16, 16384], P('groups', None, ('section', 'tp', 'seq')), parts along dimension 0, may hold values from -6 to 6
- conv_window: bfloat16 [16, 3, 16384], P('groups', None, ('section', 'tp', 'seq')), parts along dimension 0, may hold values from -6 to 6
Outputs:
- hidden_out: bfloat16 [16, 8192], P('groups', ('seq', 'section', 'tp')), parts along dimension 0
- state_out: float32 [16, 16, 16384], P('groups', None, ('section', 'tp', 'seq')), parts along dimension 0
- window_out: bfloat16 [16, 3, 16384], P('groups', None, ('section', 'tp', 'seq')), parts along dimension 0
There are 2 independent parts, one for each index of `groups`. A program takes and returns all parts, laid end to end along the dimension named above; an argument that names none is the same for every part. Nothing has to cross between parts.
Inputs may be any that keep to these rules, and one draw needn't show every extreme that they name: `lengths`: the new token sits after the cached positions; one sequence of every draw has exactly 512; where there are two or more sequences, one or two others have at most 16.
All inputs are finite; a program needn't handle non-finite values.
Results may differ from a plain program's by a relative error of at most 0.012.
Values may be sent and summed in bfloat16 or wider, within the bound.
No kernel may reach another device: no remote copies, remote signals or barrier semaphores. Data moves between devices by JAX's collectives and lax.ppermute only.
A program may use at most 192 MiB of HBM per device.

v0:
```python
import jax
import jax.numpy as jnp
from jax import lax
from jax.sharding import PartitionSpec as P

MODEL_WIDTH = 8192
QUERY_HEADS = 64
KEY_VALUE_HEADS = 8
HEAD_SIZE = 128
DS = 16
DTR = 512
EPSILON = 1e-06
NEGATIVE = -1e30


def joined(value, axis, join):
    pieces = jax.tree.map(lambda part: lax.all_gather(part, axis), value)
    head = jax.tree.map(lambda part: part[0], pieces)
    tail = jax.tree.map(lambda part: part[1:], pieces)
    subtotal, _ = lax.scan(lambda subtotal, piece: (join(subtotal, piece), None), head, tail)
    return subtotal


def combine_parts(earlier, later):
    first_max, first_sum, first_out = earlier
    second_max, second_sum, second_out = later
    largest = jnp.maximum(first_max, second_max)
    first_factor = jnp.exp(first_max - largest)
    second_factor = jnp.exp(second_max - largest)
    return (
        largest,
        first_sum * first_factor + second_sum * second_factor,
        first_out * first_factor[..., None] + second_out * second_factor[..., None],
    )


def on_device(
    hidden_in,
    lengths,
    key_value_cache,
    attn_gain,
    w_query,
    key_value_weight,
    w_output,
    mamba_gain,
    w_inproj,
    conv_weight,
    conv_bias,
    w_xproj,
    w_dtproj,
    dt_bias,
    a_log,
    d_skip,
    w_outproj,
    ssm_state,
    conv_window,
):
    batch = hidden_in.shape[0]
    seq_index = lax.axis_index("seq")
    query_groups_count = QUERY_HEADS // KEY_VALUE_HEADS
    local_kv = key_value_weight.shape[2] // HEAD_SIZE
    head_cols = local_kv * query_groups_count * HEAD_SIZE
    gathered = lax.all_gather(hidden_in, ("section", "tp"), axis=1, tiled=True)
    wide_in = gathered.astype(jnp.float32)
    normed_input = (wide_in * attn_gain).astype(jnp.bfloat16)
    square_part = jnp.sum(wide_in * wide_in, axis=1)
    query_part = jnp.dot(normed_input, w_query, preferred_element_type=jnp.float32)
    keyval_part = jnp.dot(
        normed_input,
        key_value_weight.reshape(key_value_weight.shape[0], 2 * key_value_weight.shape[2]),
        preferred_element_type=jnp.float32,
    )
    square_sum, query_sum, keyval_sum = lax.psum((square_part, query_part, keyval_part), "seq")
    reciprocal_leading = lax.rsqrt(square_sum / MODEL_WIDTH + EPSILON)
    query_rows_local = (
        (reciprocal_leading[:, None] * query_sum)
        .astype(jnp.bfloat16)
        .reshape(batch, local_kv, query_groups_count, HEAD_SIZE)
    )
    key_value_rows = (
        (reciprocal_leading[:, None] * keyval_sum)
        .astype(jnp.bfloat16)
        .reshape(batch, 2, local_kv, HEAD_SIZE)
    )
    new_key = key_value_rows[:, 0]
    new_value = key_value_rows[:, 1]
    span = key_value_cache.shape[2]
    stored_keys = key_value_cache[:, 0].reshape(batch, span, local_kv, HEAD_SIZE)
    stored_values = key_value_cache[:, 1].reshape(batch, span, local_kv, HEAD_SIZE)
    inv_root = HEAD_SIZE ** (-0.5)
    scores = (
        jnp.einsum(
            "bgrd,btgd->bgrt", query_rows_local, stored_keys, preferred_element_type=jnp.float32
        )
        * inv_root
    )
    position = seq_index * span + jnp.arange(span, dtype=jnp.int32)
    is_valid = (position[None, :] < lengths[:, None])[:, None, None, :]
    masked = jnp.where(is_valid, scores, NEGATIVE)
    local_max = jnp.max(masked, axis=3)
    weights = jnp.where(is_valid, jnp.exp(masked - local_max[..., None]), 0.0)
    local_sum = jnp.sum(weights, axis=3)
    local_out = jnp.einsum(
        "bgrt,btgd->bgrd",
        weights.astype(jnp.bfloat16),
        stored_values,
        preferred_element_type=jnp.float32,
    )
    new_score = (
        jnp.einsum("bgrd,bgd->bgr", query_rows_local, new_key, preferred_element_type=jnp.float32)
        * inv_root
    )
    value_wide = jnp.broadcast_to(
        new_value[:, :, None, :], (batch, local_kv, query_groups_count, HEAD_SIZE)
    ).astype(jnp.float32)
    new_part = (new_score, jnp.ones_like(new_score), value_wide)
    merged = joined((local_max, local_sum, local_out), "seq", combine_parts)
    top_score, denominator, numerator = combine_parts(merged, new_part)
    attended = (numerator / denominator[..., None]).astype(jnp.bfloat16).reshape(batch, head_cols)
    attn_part = jnp.dot(attended, w_output, preferred_element_type=jnp.float32)
    attn_piece = lax.psum_scatter(attn_part, ("section", "tp"), scatter_dimension=1, tiled=True)
    hidden_mid = (hidden_in.astype(jnp.float32) + attn_piece).astype(jnp.bfloat16)
    mid_rows = lax.all_gather(hidden_mid, ("section", "tp"), axis=1, tiled=True)
    mid_wide = mid_rows.astype(jnp.float32)
    mid_square = lax.psum(jnp.sum(mid_wide * mid_wide, axis=1), "seq")
    inv_second = lax.rsqrt(mid_square / MODEL_WIDTH + EPSILON)
    scaled_mid = (mid_wide * mamba_gain).astype(jnp.bfloat16)
    in_rows = w_inproj.shape[0]
    local_inner = w_inproj.shape[2]
    both_term = jnp.dot(
        scaled_mid, w_inproj.reshape(in_rows, 2 * local_inner), preferred_element_type=jnp.float32
    ).reshape(batch, 2, local_inner)
    both_sum = lax.psum_scatter(both_term, "seq", scatter_dimension=2, tiled=True)
    conv_sum = both_sum[:, 0]
    gate_sum = both_sum[:, 1]
    conv_input = (inv_second[:, None] * conv_sum).astype(jnp.bfloat16)
    window = jnp.concatenate([conv_window, conv_input[:, None, :]], axis=1)
    conv_out = conv_bias + jnp.sum(conv_weight[None] * window.astype(jnp.float32), axis=1)
    conv_act = jax.nn.silu(conv_out).astype(jnp.bfloat16)
    xproj_out = lax.psum(
        jnp.dot(conv_act, w_xproj, preferred_element_type=jnp.float32), ("seq", "section", "tp")
    )
    rate_low = xproj_out[:, :DTR].astype(jnp.bfloat16)
    input_proj = xproj_out[:, DTR : DTR + DS]
    output_proj = xproj_out[:, DTR + DS :]
    step_size = jax.nn.softplus(
        jnp.dot(rate_low, w_dtproj, preferred_element_type=jnp.float32) + dt_bias
    )
    decays = jnp.exp(-step_size[:, None, :] * jnp.exp(a_log)[None])
    conv_wide = conv_act.astype(jnp.float32)
    state_out = (
        decays * ssm_state + step_size[:, None, :] * input_proj[:, :, None] * conv_wide[:, None, :]
    )
    readout = jnp.sum(output_proj[:, :, None] * state_out, axis=1) + d_skip * conv_wide
    gate_part = inv_second[:, None] * gate_sum
    gated_out = (readout * jax.nn.silu(gate_part)).astype(jnp.bfloat16)
    mamba_part = jnp.dot(
        lax.all_gather(gated_out, "seq", axis=1, tiled=True),
        w_outproj,
        preferred_element_type=jnp.float32,
    )
    mamba_piece = lax.psum_scatter(mamba_part, ("section", "tp"), scatter_dimension=1, tiled=True)
    hidden_out = (hidden_mid.astype(jnp.float32) + mamba_piece).astype(jnp.bfloat16)
    return (hidden_out, state_out, window[:, 1:])


def solution(mesh):
    return jax.shard_map(
        on_device,
        mesh=mesh,
        in_specs=(
            P("groups", ("seq", "section", "tp")),
            P("groups"),
            P("groups", None, "seq", ("section", "tp")),
            P("seq"),
            P("seq", ("section", "tp")),
            P("seq", None, ("section", "tp")),
            P(("section", "tp"), "seq"),
            P("seq"),
            P("seq", None, ("section", "tp")),
            P(None, ("section", "tp", "seq")),
            P(("section", "tp", "seq")),
            P(("section", "tp", "seq"), None),
            P(None, ("section", "tp", "seq")),
            P(("section", "tp", "seq")),
            P(None, ("section", "tp", "seq")),
            P(("section", "tp", "seq")),
            P(("section", "tp"), "seq"),
            P("groups", None, ("section", "tp", "seq")),
            P("groups", None, ("section", "tp", "seq")),
        ),
        out_specs=(
            P("groups", ("seq", "section", "tp")),
            P("groups", None, ("section", "tp", "seq")),
            P("groups", None, ("section", "tp", "seq")),
        ),
        check_vma=False,
    )
```

profile of v0, /device:TPU:0, one launch (start us, length us, event | category | flops | bytes accessed | tf_op | source)
XLA Modules:
  0.0 326.4 jit_solution(9584996585662456472)
XLA Ops:
  7.2 0.0 copy-start
  7.2 0.0 all-reduce.3.cloned.1.call-start
  7.2 6.5 %all_gather.27 = bf16[8,2048]{1,0:T(8,128)(2,1)S(1)} all-gather(bf16[8,512]{1,0:T(8,128)(2,1)} %param.21), channel_id=1, replica_groups=mesh['groups'=2,'seq'=4,'section'=2,'tp'=2] {'section','tp'}, dimensions={1}, use_global_device_ids=true | all-gather | bytes 40960 | tf_op jit(solution)/shard_map/all_gather | solution.py:63
  13.8 5.4 %fusion.32 = f32[8,2048]{1,0:T(8,128)} fusion(bf16[2048,2048]{1,0:T(8,128)(2,1)} %param.25, bf16[8,2048]{1,0:T(8,128)(2,1)S(1)} %all_gather.27, f32[2048]{0:T(1024)} %param.24), kind=kOutput, calls=%fused_computation.56 | convolution fusion | flops 67158016 | bytes 8495104 | tf_op jit(solution)/shard_map/dot_general | solution.py:67
  19.1 0.0 all-reduce.3.cloned.1.call-update
  19.2 0.0 reduce-scatter.4.cloned.1.call-start
  19.2 0.1 fusion.5
  19.3 2.3 fusion.43
  21.6 0.4 copy.96
  22.1 0.0 copy-done.5
  22.1 0.4 fusion.30
  22.4 19.7 %all-reduce = (f32[8]{0:T(128)S(1)}, f32[8,512]{1,0:T(8,128)S(1)}) all-reduce(f32[8]{0:T(128)S(1)} %fusion.5, f32[8,512]{1,0:T(8,128)S(1)} %fusion.30), channel_id=1, replica_groups=mesh['groups'=2,'seq'=4,'section'=2,'tp'=2] {'seq'}, use_global_device_ids=true, to_apply=%region_1.0 | all-reduce | flops 4104 | bytes 32832 | tf_op jit(solution)/shard_map/psum | solution.py:73
  42.1 0.1 multiply_convert_fusion.3
  42.2 0.0 copy-done.13
  42.2 0.1 broadcast_compare_fusion
  42.3 1.3 copy.94
  43.6 1.3 copy.95
  44.9 10.5 %all-reduce.3.cloned.1.call-done = f32[8,2048]{1,0:T(8,128)} async-done(((f32[8,2048]{1,0:T(8,128)}), f32[8,2048]{1,0:T(8,128)}) %all-reduce.3.cloned.1.call-update) | async-done | bytes 65552 | tf_op jit(solution)/shard_map/psum | solution.py:73
  55.4 0.9 multiply_convert_fusion
  56.3 0.3 fusion.45
  56.6 13.1 %all-gather = f32[32,2,8]{2,1,0:T(2,128)S(1)} all-gather(f32[8,2,8]{2,1,0:T(2,128)S(1)} %get-tuple-element.101), channel_id=2, replica_groups=mesh['groups'=2,'seq'=4,'section'=2,'tp'=2] {'seq'}, dimensions={0}, use_global_device_ids=true | all-gather | bytes 2560 | tf_op jit(solution)/shard_map/all_gather | solution.py:17
  69.8 0.2 fusion.10
  70.0 13.2 %all-gather.1 = f32[32,2,8]{2,1,0:T(2,128)S(1)} all-gather(f32[8,2,8]{2,1,0:T(2,128)S(1)} %fusion.10), channel_id=3, replica_groups=mesh['groups'=2,'seq'=4,'section'=2,'tp'=2] {'seq'}, dimensions={0}, use_global_device_ids=true | all-gather | bytes 2560 | tf_op jit(solution)/shard_map/all_gather | solution.py:17
  83.2 0.4 fusion.12
  83.6 13.8 %all-gather.2 = f32[32,2,8,128]{3,2,1,0:T(8,128)S(1)} all-gather(f32[8,2,8,128]{3,2,1,0:T(8,128)S(1)} %fusion.12), channel_id=4, replica_groups=mesh['groups'=2,'seq'=4,'section'=2,'tp'=2] {'seq'}, dimensions={0}, use_global_device_ids=true | all-gather | bytes 327680 | tf_op jit(solution)/shard_map/all_gather | solution.py:17
  97.4 0.6 while.14
  97.5 0.1 fusion.63
  97.7 0.1 fusion.63
  97.9 0.1 fusion.63
  98.0 0.1 fusion.27
  98.2 0.1 fusion.25
  98.3 5.2 %fusion.17 = f32[8,2048]{1,0:T(8,128)} fusion(bf16[2048,2048]{1,0:T(8,128)(2,1)} %param.27, bf16[1,8,16,128]{3,2,1,0:T(8,128)(2,1)S(1)} %fusion.25), kind=kOutput, calls=%fused_computation.38 | convolution fusion | flops 67108864 | bytes 8486912 | tf_op jit(solution)/shard_map/dot_general | solution.py:120
  103.5 0.0 reduce-scatter.4.cloned.1.call-update
  103.6 0.0 reduce-scatter.6.cloned.1.call-start
  103.6 29.5 %copy.98 = bf16[256,8,2,4096]{3,1,2,0:T(8,128)(2,1)} copy(bf16[256,8,2,4096]{3,2,1,0:T(2,128)(2,1)} %bitcast.80) | data formatting | bytes 67108864
  133.1 44.5 %copy.83 = bf16[8192,2048]{1,0:T(8,128)(2,1)} copy(bf16[8192,2048]{0,1:T(8,128)(2,1)} %bitcast.79) | data formatting | bytes 67108864 | tf_op jit(solution)/shard_map/dot_general | solution.py:130
  177.6 0.7 add_convert_fusion.1
  178.3 5.2 %all_gather.34 = bf16[8,2048]{1,0:T(8,128)(2,1)S(1)} all-gather(bf16[8,512]{1,0:T(8,128)(2,1)S(1)} %add_convert_fusion.1), channel_id=1, replica_groups=mesh['groups'=2,'seq'=4,'section'=2,'tp'=2] {'section','tp'}, dimensions={1}, use_global_device_ids=true | all-gather | bytes 40960 | tf_op jit(solution)/shard_map/all_gather | solution.py:123
  183.5 0.0 copy-start.12
  183.5 0.0 copy-start.2
  183.5 0.0 copy-start.10
  183.6 0.0 copy-start.3
  183.6 0.0 copy-start.11
  183.6 14.8 %fusion.15 = f32[8,2,4096]{2,0,1:T(8,128)} fusion(bf16[2,4096,2048]{2,1,0:T(8,128)(2,1)} %bitcast.78, bf16[8,2048]{1,0:T(8,128)(2,1)S(1)} %all_gather.34, f32[2048]{0:T(1024)S(1)} %copy-done.7), kind=kOutput, calls=%fused_computation.37 | convolution fusion | flops 268484608 | bytes 33857536 | tf_op jit(solution)/shard_map/dot_general | solution.py:130
  198.4 0.0 reduce-scatter.6.cloned.1.call-update
  198.4 0.0 reduce-scatter.8.cloned.1.call-start
  198.5 0.1 fusion.7
  198.6 10.6 %psum.38 = f32[8]{0:T(128)S(1)} all-reduce(f32[8]{0:T(128)S(1)} %fusion.7), channel_id=1, replica_groups=mesh['groups'=2,'seq'=4,'section'=2,'tp'=2] {'seq'}, use_global_device_ids=true, to_apply=%region_10.11 | all-reduce | flops 8 | bytes 64 | tf_op jit(solution)/shard_map/psum | solution.py:125
  209.2 9.1 %reduce-scatter.6.cloned.1.call-done = f32[8,2,1024]{2,0,1:T(8,128)} async-done(((f32[8,2,4096]{2,0,1:T(8,128)}), f32[8,2,1024]{2,0,1:T(8,128)}) %reduce-scatter.6.cloned.1.call-update) | async-done | bytes 65552 | tf_op jit(solution)/shard_map/reduce_scatter | solution.py:133
  218.3 0.8 fusion.21
  219.2 0.0 copy-done.4
  219.2 0.0 copy-done.12
  219.2 0.4 fusion.47
  219.6 57.6 %psum.39 = f32[8,544]{1,0:T(8,128)S(1)} all-reduce(f32[8,544]{1,0:T(8,128)S(1)} %fusion.47), channel_id=1, replica_groups=mesh['groups'=2,'seq'=4,'section'=2,'tp'=2] {'seq','section','tp'}, use_global_device_ids=true, to_apply=%region_13.14 | all-reduce | flops 4352 | bytes 34816 | tf_op jit(solution)/shard_map/psum | solution.py:140
  277.3 0.1 fusion.44
  277.4 0.3 fusion.46
  277.6 1.1 multiply_reduce_fusion
  278.7 0.8 multiply_convert_fusion.1
  279.6 13.3 %all_gather.35 = bf16[8,4096]{1,0:T(8,128)(2,1)S(1)} all-gather(bf16[8,1024]{1,0:T(8,128)(2,1)S(1)} %multiply_convert_fusion.1), channel_id=1, replica_groups=mesh['groups'=2,'seq'=4,'section'=2,'tp'=2] {'seq'}, dimensions={1}, use_global_device_ids=true | all-gather | bytes 81920 | tf_op jit(solution)/shard_map/all_gather | solution.py:158
  292.9 8.7 %fusion.48 = f32[8,2048]{1,0:T(8,128)} fusion(bf16[8,4096]{1,0:T(8,128)(2,1)S(1)} %all_gather.35, bf16[4096,2048]{1,0:T(8,128)(2,1)} %param.37), kind=kOutput, calls=%fused_computation.82 | convolution fusion | flops 134217728 | bytes 16908288 | tf_op jit(solution)/shard_map/dot_general | solution.py:157
  301.6 0.0 reduce-scatter.8.cloned.1.call-update
  301.6 0.6 fusion.11
  302.2 16.3 %reduce-scatter.8.cloned.1.call-done = f32[8,512]{1,0:T(8,128)} async-done(((f32[8,2048]{1,0:T(8,128)}), f32[8,512]{1,0:T(8,128)}) %reduce-scatter.8.cloned.1.call-update) | async-done | bytes 16400 | tf_op jit(solution)/shard_map/reduce_scatter | solution.py:162
  318.5 1.3 add_convert_fusion
  (51 shorter events, 0.3 us)
Async XLA Ops:
  7.2 212.1 %copy-start = (bf16[1024,544]{0,1:T(8,128)(2,1)S(1)}, bf16[1024,544]{0,1:T(8,128)(2,1)}, u32[]{:S(2)}) copy-start(bf16[1024,544]{0,1:T(8,128)(2,1)} %param.32) | copy-start | bytes 3342340
  7.2 48.2 %all-reduce.3.cloned.1.call-start = ((), (), s32[]{:S(2)}) async-start(), calls=%async_computation.3 | async-start | bytes 131072 | tf_op jit(solution)/shard_map/psum | solution.py:73
  13.8 7.8 %copy-start.1 = (bf16[2048,2,256]{2,1,0:T(2,128)(2,1)S(1)}, bf16[2048,2,256]{2,1,0:T(2,128)(2,1)}, u32[]{:S(2)}) copy-start(bf16[2048,2,256]{2,1,0:T(2,128)(2,1)} %param.26) | copy-start | bytes 6291460
  13.8 8.3 %copy-start.5 = (f32[2048]{0:T(1024)S(1)}, f32[2048]{0:T(1024)}, u32[]{:S(2)}) copy-start(f32[2048]{0:T(1024)} %param.24) | copy-start | bytes 24580
  13.8 28.4 %copy-start.13 = (s32[8]{0:T(128)S(1)}, s32[8]{0:T(128)}, u32[]{:S(2)}) copy-start(s32[8]{0:T(128)} %param.22) | copy-start | bytes 100
  19.2 158.4 %reduce-scatter.4.cloned.1.call-start = ((), (), s32[]{:S(2)}) async-start(), calls=%async_computation.4 | async-start | bytes 81920 | tf_op jit(solution)/shard_map/reduce_scatter | solution.py:121
  103.6 114.8 %reduce-scatter.6.cloned.1.call-start = ((), (), s32[]{:S(2)}) async-start(), calls=%async_computation.5 | async-start | bytes 327680 | tf_op jit(solution)/shard_map/reduce_scatter | solution.py:133
  133.1 44.5 %copy-start.8 = (bf16[8,512]{1,0:T(8,128)(2,1)S(1)}, bf16[8,512]{1,0:T(8,128)(2,1)}, u32[]{:S(2)}) copy-start(bf16[8,512]{1,0:T(8,128)(2,1)} %param.21) | copy-start | bytes 24580
  133.1 50.4 %copy-start.7 = (f32[2048]{0:T(1024)S(1)}, f32[2048]{0:T(1024)}, u32[]{:S(2)}) copy-start(f32[2048]{0:T(1024)} %param.28) | copy-start | bytes 24580
  183.5 15.1 %copy-start.6 = (f32[16,1024]{1,0:T(8,128)S(1)}, f32[16,1024]{1,0:T(8,128)}, u32[]{:S(2)}) copy-start(f32[16,1024]{1,0:T(8,128)} %param.35) | copy-start | bytes 196612
  183.5 35.7 %copy-start.4 = (bf16[8,3,1024]{2,0,1:T(8,128)(2,1)S(1)}, bf16[8,3,1024]{2,0,1:T(8,128)(2,1)}, u32[]{:S(2)}) copy-start(bf16[8,3,1024]{2,0,1:T(8,128)(2,1)} %param.39) | copy-start | bytes 147460
  183.5 35.7 %copy-start.9 = (f32[4,1024]{1,0:T(4,128)S(1)}, f32[4,1024]{1,0:T(4,128)}, u32[]{:S(2)}) copy-start(f32[4,1024]{1,0:T(4,128)} %param.30) | copy-start | bytes 49156
  183.5 35.7 %copy-start.12 = (f32[1024]{0:T(1024)S(1)}, f32[1024]{0:T(1024)}, u32[]{:S(2)}) copy-start(f32[1024]{0:T(1024)} %param.31) | copy-start | bytes 12292
  183.5 93.8 %copy-start.2 = (bf16[512,1024]{1,0:T(8,128)(2,1)S(1)}, bf16[512,1024]{1,0:T(8,128)(2,1)}, u32[]{:S(2)}) copy-start(bf16[512,1024]{1,0:T(8,128)(2,1)} %param.33) | copy-start | bytes 3145732
  183.5 93.8 %copy-start.10 = (f32[1024]{0:T(1024)S(1)}, f32[1024]{0:T(1024)}, u32[]{:S(2)}) copy-start(f32[1024]{0:T(1024)} %param.34) | copy-start | bytes 12292
  183.6 94.1 %copy-start.3 = (f32[8,16,1024]{2,1,0:T(8,128)S(1)}, f32[8,16,1024]{2,1,0:T(8,128)}, u32[]{:S(2)}) copy-start(f32[8,16,1024]{2,1,0:T(8,128)} %param.38) | copy-start | bytes 1572868
  183.6 95.2 %copy-start.11 = (f32[1024]{0:T(1024)S(1)}, f32[1024]{0:T(1024)}, u32[]{:S(2)}) copy-start(f32[1024]{0:T(1024)} %param.36) | copy-start | bytes 12292
  198.4 120.1 %reduce-scatter.8.cloned.1.call-start = ((), (), s32[]{:S(2)}) async-start(), calls=%async_computation.6 | async-start | bytes 81920 | tf_op jit(solution)/shard_map/reduce_scatter | solution.py:162
Sparse Core Ops, SparseCore 0:
  19.3 36.0 all-reduce.2
  103.7 19.3 reduce-scatter.3
  198.5 19.7 reduce-scatter.5
  301.7 16.7 reduce-scatter.7
where the time goes:
time: 328 us; the launch traced here: 326 us
  blocking collectives  153 us (47%)
  local copies, waits for them, and re-layouts  79.6 us (24%)
  waiting for transfers between devices  36 us (11%)
  matrix products  35.9 us (11%)
  between operations  14 us (4%)
  other arithmetic  7.51 us (2%)
    psum x1, blocking collectives, on_device(): lax.psum(jnp.dot(conv_act, w_xproj, preferred_element_type=jnp.float32),...  57.6 us
    dot_general x1, local copies, waits for them, and re-layouts, on_device(): jnp.dot(scaled_mid, w_inproj.reshape(in_rows, 2 * local_inner), preferred...  44.5 us
    all_gather x3, blocking collectives, joined(): pieces = jax.tree.map(lambda part: lax.all_gather(part, axis), value)  40.1 us
    unnamed x32, local copies, waits for them, and re-layouts  32.7 us
    psum x1, blocking collectives, on_device(): lax.psum((square_part, query_part, keyval_part), 'seq')  19.7 us
    reduce_scatter x1, waiting for transfers between devices, on_device(): lax.psum_scatter(mamba_part, ('section', 'tp'), scatter_dimension=1, tile...  16.3 us
    dot_general x1, matrix products, on_device(): jnp.dot(scaled_mid, w_inproj.reshape(in_rows, 2 * local_inner), preferred...  14.8 us
    all_gather x1, blocking collectives, on_device(): lax.all_gather(gated_out, 'seq', axis=1, tiled=True)  13.3 us
  transfers between devices with their start and end apart: 4, of which 3 were waited for; matrix products, arithmetic and copies ran while one was open for 25% of the time, Pallas kernels for 0%

commit v1 on v0

--- a/solution.py
+++ b/solution.py
@@ -137,8 +137,11 @@
     window = jnp.concatenate([conv_window, conv_input[:, None, :]], axis=1)
     conv_out = conv_bias + jnp.sum(conv_weight[None] * window.astype(jnp.float32), axis=1)
     conv_act = jax.nn.silu(conv_out).astype(jnp.bfloat16)
-    xproj_out = lax.psum(
-        jnp.dot(conv_act, w_xproj, preferred_element_type=jnp.float32), ("seq", "section", "tp")
+    xproj_out = jnp.sum(
+        lax.all_gather(
+            jnp.dot(conv_act, w_xproj, preferred_element_type=jnp.float32), ("seq", "section", "tp")
+        ),
+        axis=0,
     )
     rate_low = xproj_out[:, :DTR].astype(jnp.bfloat16)
     input_proj = xproj_out[:, DTR : DTR + DS]

time: 328 us -> 290 us (0.88)
  blocking collectives: 153 us -> 115 us
    psum x1 -> x0, blocking collectives: 57.6 us -> none  [on_device(): lax.psum(jnp.dot(conv_act, w_xproj, preferred_element_type=jnp.float32),...]
    all_gather x0 -> x1, blocking collectives: none -> 19.4 us  [on_device(): lax.all_gather(jnp.dot(conv_act, w_xproj, preferred_element_type=jnp.floa...]
  transfers between devices with their start and end apart: 4 -> 4, of which waited for: 3 -> 3; matrix products, arithmetic and copies ran while one was open for 25% -> 28% of each run, Pallas kernels for 0% -> 0%
where the time goes in v1:
time: 290 us; the launch traced here: 288 us
  blocking collectives  115 us (40%)
  local copies, waits for them, and re-layouts  79.6 us (27%)
  waiting for transfers between devices  36.1 us (12%)
  matrix products  35.9 us (12%)
  between operations  14 us (5%)
  other arithmetic  7.54 us (3%)
    dot_general x1, local copies, waits for them, and re-layouts, on_device(): jnp.dot(scaled_mid, w_inproj.reshape(in_rows, 2 * local_inner), preferred...  44.5 us
    all_gather x3, blocking collectives, joined(): pieces = jax.tree.map(lambda part: lax.all_gather(part, axis), value)  40.1 us
    unnamed x32, local copies, waits for them, and re-layouts  32.7 us
    psum x1, blocking collectives, on_device(): lax.psum((square_part, query_part, keyval_part), 'seq')  19.7 us
    all_gather x1, blocking collectives, on_device(): lax.all_gather(jnp.dot(conv_act, w_xproj, preferred_element_type=jnp.floa...  19.4 us
    reduce_scatter x1, waiting for transfers between devices, on_device(): lax.psum_scatter(mamba_part, ('section', 'tp'), scatter_dimension=1, tile...  16.4 us
    dot_general x1, matrix products, on_device(): jnp.dot(scaled_mid, w_inproj.reshape(in_rows, 2 * local_inner), preferred...  14.8 us
    all_gather x1, blocking collectives, on_device(): lax.all_gather(gated_out, 'seq', axis=1, tiled=True)  13.3 us
  transfers between devices with their start and end apart: 4, of which 3 were waited for; matrix products, arithmetic and copies ran while one was open for 28% of the time, Pallas kernels for 0%

profile of v1, /device:TPU:0, one launch (start us, length us, event | category | flops | bytes accessed | tf_op | source)
XLA Modules:
  0.0 288.3 jit_solution(14254712098349582015)
XLA Ops:
  7.2 0.0 copy-start
  7.2 0.0 all-reduce.3.cloned.1.call-start
  7.2 6.5 %all_gather.33 = bf16[8,2048]{1,0:T(8,128)(2,1)S(1)} all-gather(bf16[8,512]{1,0:T(8,128)(2,1)} %param.21), channel_id=1, replica_groups=mesh['groups'=2,'seq'=4,'section'=2,'tp'=2] {'section','tp'}, dimensions={1}, use_global_device_ids=true | all-gather | bytes 40960 | tf_op jit(solution)/shard_map/all_gather | solution.py:63
  13.8 5.4 %fusion.32 = f32[8,2048]{1,0:T(8,128)} fusion(bf16[2048,2048]{1,0:T(8,128)(2,1)} %param.25, bf16[8,2048]{1,0:T(8,128)(2,1)S(1)} %all_gather.33, f32[2048]{0:T(1024)} %param.24), kind=kOutput, calls=%fused_computation.57 | convolution fusion | flops 67158016 | bytes 8495104 | tf_op jit(solution)/shard_map/dot_general | solution.py:67
  19.1 0.0 all-reduce.3.cloned.1.call-update
  19.2 0.0 reduce-scatter.4.cloned.1.call-start
  19.2 0.1 fusion.5
  19.3 2.3 fusion.43
  21.6 0.4 copy.96
  22.1 0.0 copy-done.5
  22.1 0.4 fusion.30
  22.4 19.7 %all-reduce = (f32[8]{0:T(128)S(1)}, f32[8,512]{1,0:T(8,128)S(1)}) all-reduce(f32[8]{0:T(128)S(1)} %fusion.5, f32[8,512]{1,0:T(8,128)S(1)} %fusion.30), channel_id=1, replica_groups=mesh['groups'=2,'seq'=4,'section'=2,'tp'=2] {'seq'}, use_global_device_ids=true, to_apply=%region_1.0 | all-reduce | flops 4104 | bytes 32832 | tf_op jit(solution)/shard_map/psum | solution.py:73
  42.1 0.1 multiply_convert_fusion.3
  42.2 0.0 copy-done.13
  42.2 0.1 broadcast_compare_fusion
  42.3 1.3 copy.94
  43.6 1.3 copy.95
  44.9 10.5 %all-reduce.3.cloned.1.call-done = f32[8,2048]{1,0:T(8,128)} async-done(((f32[8,2048]{1,0:T(8,128)}), f32[8,2048]{1,0:T(8,128)}) %all-reduce.3.cloned.1.call-update) | async-done | bytes 65552 | tf_op jit(solution)/shard_map/psum | solution.py:73
  55.4 0.9 multiply_convert_fusion
  56.3 0.3 fusion.45
  56.6 13.1 %all-gather = f32[32,2,8]{2,1,0:T(2,128)S(1)} all-gather(f32[8,2,8]{2,1,0:T(2,128)S(1)} %get-tuple-element.101), channel_id=2, replica_groups=mesh['groups'=2,'seq'=4,'section'=2,'tp'=2] {'seq'}, dimensions={0}, use_global_device_ids=true | all-gather | bytes 2560 | tf_op jit(solution)/shard_map/all_gather | solution.py:17
  69.8 0.2 fusion.10
  70.0 13.2 %all-gather.1 = f32[32,2,8]{2,1,0:T(2,128)S(1)} all-gather(f32[8,2,8]{2,1,0:T(2,128)S(1)} %fusion.10), channel_id=3, replica_groups=mesh['groups'=2,'seq'=4,'section'=2,'tp'=2] {'seq'}, dimensions={0}, use_global_device_ids=true | all-gather | bytes 2560 | tf_op jit(solution)/shard_map/all_gather | solution.py:17
  83.2 0.4 fusion.12
  83.6 13.8 %all-gather.2 = f32[32,2,8,128]{3,2,1,0:T(8,128)S(1)} all-gather(f32[8,2,8,128]{3,2,1,0:T(8,128)S(1)} %fusion.12), channel_id=4, replica_groups=mesh['groups'=2,'seq'=4,'section'=2,'tp'=2] {'seq'}, dimensions={0}, use_global_device_ids=true | all-gather | bytes 327680 | tf_op jit(solution)/shard_map/all_gather | solution.py:17
  97.4 0.6 while.14
  97.5 0.1 fusion.63
  97.7 0.1 fusion.63
  97.9 0.1 fusion.63
  98.0 0.1 fusion.27
  98.2 0.1 fusion.25
  98.3 5.2 %fusion.17 = f32[8,2048]{1,0:T(8,128)} fusion(bf16[2048,2048]{1,0:T(8,128)(2,1)} %param.27, bf16[1,8,16,128]{3,2,1,0:T(8,128)(2,1)S(1)} %fusion.25), kind=kOutput, calls=%fused_computation.39 | convolution fusion | flops 67108864 | bytes 8486912 | tf_op jit(solution)/shard_map/dot_general | solution.py:120
  103.5 0.0 reduce-scatter.4.cloned.1.call-update
  103.6 0.0 reduce-scatter.6.cloned.1.call-start
  103.6 29.5 %copy.98 = bf16[256,8,2,4096]{3,1,2,0:T(8,128)(2,1)} copy(bf16[256,8,2,4096]{3,2,1,0:T(2,128)(2,1)} %bitcast.82) | data formatting | bytes 67108864
  133.1 44.5 %copy.83 = bf16[8192,2048]{1,0:T(8,128)(2,1)} copy(bf16[8192,2048]{0,1:T(8,128)(2,1)} %bitcast.81) | data formatting | bytes 67108864 | tf_op jit(solution)/shard_map/dot_general | solution.py:130
  177.6 0.7 add_convert_fusion.1
  178.3 5.2 %all_gather.40 = bf16[8,2048]{1,0:T(8,128)(2,1)S(1)} all-gather(bf16[8,512]{1,0:T(8,128)(2,1)S(1)} %add_convert_fusion.1), channel_id=1, replica_groups=mesh['groups'=2,'seq'=4,'section'=2,'tp'=2] {'section','tp'}, dimensions={1}, use_global_device_ids=true | all-gather | bytes 40960 | tf_op jit(solution)/shard_map/all_gather | solution.py:123
  183.5 0.0 copy-start.12
  183.5 0.0 copy-start.2
  183.5 0.0 copy-start.10
  183.6 0.0 copy-start.3
  183.6 0.0 copy-start.11
  183.6 14.8 %fusion.15 = f32[8,2,4096]{2,0,1:T(8,128)} fusion(bf16[2,4096,2048]{2,1,0:T(8,128)(2,1)} %bitcast.80, bf16[8,2048]{1,0:T(8,128)(2,1)S(1)} %all_gather.40, f32[2048]{0:T(1024)S(1)} %copy-done.7), kind=kOutput, calls=%fused_computation.38 | convolution fusion | flops 268484608 | bytes 33857536 | tf_op jit(solution)/shard_map/dot_general | solution.py:130
  198.4 0.0 reduce-scatter.6.cloned.1.call-update
  198.4 0.0 reduce-scatter.8.cloned.1.call-start
  198.5 0.1 fusion.7
  198.6 10.6 %psum.31 = f32[8]{0:T(128)S(1)} all-reduce(f32[8]{0:T(128)S(1)} %fusion.7), channel_id=1, replica_groups=mesh['groups'=2,'seq'=4,'section'=2,'tp'=2] {'seq'}, use_global_device_ids=true, to_apply=%region_10.11 | all-reduce | flops 8 | bytes 64 | tf_op jit(solution)/shard_map/psum | solution.py:125
  209.2 9.1 %reduce-scatter.6.cloned.1.call-done = f32[8,2,1024]{2,0,1:T(8,128)} async-done(((f32[8,2,4096]{2,0,1:T(8,128)}), f32[8,2,1024]{2,0,1:T(8,128)}) %reduce-scatter.6.cloned.1.call-update) | async-done | bytes 65552 | tf_op jit(solution)/shard_map/reduce_scatter | solution.py:133
  218.3 0.8 fusion.21
  219.2 0.0 copy-done.4
  219.2 0.0 copy-done.12
  219.2 0.4 fusion.47
  219.6 19.4 %all-gather.3 = f32[128,544]{1,0:T(8,128)S(1)} all-gather(f32[8,544]{1,0:T(8,128)S(1)} %fusion.47), channel_id=5, replica_groups=mesh['groups'=2,'seq'=4,'section'=2,'tp'=2] {'seq','section','tp'}, dimensions={0}, use_global_device_ids=true | all-gather | bytes 295936 | tf_op jit(solution)/shard_map/all_gather | solution.py:141
  239.1 0.1 fusion.44
  239.2 0.3 fusion.46
  239.5 1.1 multiply_reduce_fusion
  240.6 0.8 multiply_convert_fusion.1
  241.4 13.3 %all_gather.43 = bf16[8,4096]{1,0:T(8,128)(2,1)S(1)} all-gather(bf16[8,1024]{1,0:T(8,128)(2,1)S(1)} %multiply_convert_fusion.1), channel_id=1, replica_groups=mesh['groups'=2,'seq'=4,'section'=2,'tp'=2] {'seq'}, dimensions={1}, use_global_device_ids=true | all-gather | bytes 81920 | tf_op jit(solution)/shard_map/all_gather | solution.py:161
  254.7 8.7 %fusion.48 = f32[8,2048]{1,0:T(8,128)} fusion(bf16[8,4096]{1,0:T(8,128)(2,1)S(1)} %all_gather.43, bf16[4096,2048]{1,0:T(8,128)(2,1)} %param.37), kind=kOutput, calls=%fused_computation.83 | convolution fusion | flops 134217728 | bytes 16908288 | tf_op jit(solution)/shard_map/dot_general | solution.py:160
  263.4 0.0 reduce-scatter.8.cloned.1.call-update
  263.4 0.6 fusion.11
  264.0 16.4 %reduce-scatter.8.cloned.1.call-done = f32[8,512]{1,0:T(8,128)} async-done(((f32[8,2048]{1,0:T(8,128)}), f32[8,512]{1,0:T(8,128)}) %reduce-scatter.8.cloned.1.call-update) | async-done | bytes 16400 | tf_op jit(solution)/shard_map/reduce_scatter | solution.py:165
  280.5 1.3 add_convert_fusion
  (52 shorter events, 0.3 us)
Async XLA Ops:
  7.2 212.1 %copy-start = (bf16[1024,544]{0,1:T(8,128)(2,1)S(1)}, bf16[1024,544]{0,1:T(8,128)(2,1)}, u32[]{:S(2)}) copy-start(bf16[1024,544]{0,1:T(8,128)(2,1)} %param.32) | copy-start | bytes 3342340
  7.2 48.2 %all-reduce.3.cloned.1.call-start = ((), (), s32[]{:S(2)}) async-start(), calls=%async_computation.3 | async-start | bytes 131072 | tf_op jit(solution)/shard_map/psum | solution.py:73
  13.8 7.8 %copy-start.1 = (bf16[2048,2,256]{2,1,0:T(2,128)(2,1)S(1)}, bf16[2048,2,256]{2,1,0:T(2,128)(2,1)}, u32[]{:S(2)}) copy-start(bf16[2048,2,256]{2,1,0:T(2,128)(2,1)} %param.26) | copy-start | bytes 6291460
  13.8 8.3 %copy-start.5 = (f32[2048]{0:T(1024)S(1)}, f32[2048]{0:T(1024)}, u32[]{:S(2)}) copy-start(f32[2048]{0:T(1024)} %param.24) | copy-start | bytes 24580
  13.8 28.4 %copy-start.13 = (s32[8]{0:T(128)S(1)}, s32[8]{0:T(128)}, u32[]{:S(2)}) copy-start(s32[8]{0:T(128)} %param.22) | copy-start | bytes 100
  19.2 158.4 %reduce-scatter.4.cloned.1.call-start = ((), (), s32[]{:S(2)}) async-start(), calls=%async_computation.4 | async-start | bytes 81920 | tf_op jit(solution)/shard_map/reduce_scatter | solution.py:121
  103.6 114.8 %reduce-scatter.6.cloned.1.call-start = ((), (), s32[]{:S(2)}) async-start(), calls=%async_computation.5 | async-start | bytes 327680 | tf_op jit(solution)/shard_map/reduce_scatter | solution.py:133
  133.1 44.5 %copy-start.8 = (bf16[8,512]{1,0:T(8,128)(2,1)S(1)}, bf16[8,512]{1,0:T(8,128)(2,1)}, u32[]{:S(2)}) copy-start(bf16[8,512]{1,0:T(8,128)(2,1)} %param.21) | copy-start | bytes 24580
  133.1 50.4 %copy-start.7 = (f32[2048]{0:T(1024)S(1)}, f32[2048]{0:T(1024)}, u32[]{:S(2)}) copy-start(f32[2048]{0:T(1024)} %param.28) | copy-start | bytes 24580
  183.5 15.1 %copy-start.6 = (f32[16,1024]{1,0:T(8,128)S(1)}, f32[16,1024]{1,0:T(8,128)}, u32[]{:S(2)}) copy-start(f32[16,1024]{1,0:T(8,128)} %param.35) | copy-start | bytes 196612
  183.5 35.7 %copy-start.4 = (bf16[8,3,1024]{2,0,1:T(8,128)(2,1)S(1)}, bf16[8,3,1024]{2,0,1:T(8,128)(2,1)}, u32[]{:S(2)}) copy-start(bf16[8,3,1024]{2,0,1:T(8,128)(2,1)} %param.39) | copy-start | bytes 147460
  183.5 35.7 %copy-start.9 = (f32[4,1024]{1,0:T(4,128)S(1)}, f32[4,1024]{1,0:T(4,128)}, u32[]{:S(2)}) copy-start(f32[4,1024]{1,0:T(4,128)} %param.30) | copy-start | bytes 49156
  183.5 35.7 %copy-start.12 = (f32[1024]{0:T(1024)S(1)}, f32[1024]{0:T(1024)}, u32[]{:S(2)}) copy-start(f32[1024]{0:T(1024)} %param.31) | copy-start | bytes 12292
  183.5 55.7 %copy-start.2 = (bf16[512,1024]{1,0:T(8,128)(2,1)S(1)}, bf16[512,1024]{1,0:T(8,128)(2,1)}, u32[]{:S(2)}) copy-start(bf16[512,1024]{1,0:T(8,128)(2,1)} %param.33) | copy-start | bytes 3145732
  183.5 55.6 %copy-start.10 = (f32[1024]{0:T(1024)S(1)}, f32[1024]{0:T(1024)}, u32[]{:S(2)}) copy-start(f32[1024]{0:T(1024)} %param.34) | copy-start | bytes 12292
  183.6 55.9 %copy-start.3 = (f32[8,16,1024]{2,1,0:T(8,128)S(1)}, f32[8,16,1024]{2,1,0:T(8,128)}, u32[]{:S(2)}) copy-start(f32[8,16,1024]{2,1,0:T(8,128)} %param.38) | copy-start | bytes 1572868
  183.6 57.0 %copy-start.11 = (f32[1024]{0:T(1024)S(1)}, f32[1024]{0:T(1024)}, u32[]{:S(2)}) copy-start(f32[1024]{0:T(1024)} %param.36) | copy-start | bytes 12292
  198.4 82.1 %reduce-scatter.8.cloned.1.call-start = ((), (), s32[]{:S(2)}) async-start(), calls=%async_computation.6 | async-start | bytes 81920 | tf_op jit(solution)/shard_map/reduce_scatter | solution.py:165
Sparse Core Ops, SparseCore 0:
  19.3 36.0 all-reduce.2
  103.7 19.3 reduce-scatter.3
  198.5 19.7 reduce-scatter.5
  263.5 16.8 reduce-scatter.7
